TPU v7x, 256 devices: a whole 4x4x8 slice. The times are simulated.
256 devices in a mesh: prow: 16 (over z, core), pcol: 16 (over y, x).
Axes of the slice: x: 4, y: 4, z: 8, core: 2. Of those that a mesh axis runs over, the one named last changes fastest.
Arguments:
- root_inverse: float32 [2, 16, 128, 2, 16, 128], P(None, 'prow', None, None, 'pcol'), as said below
- lower_one: float32 [2, 16, 128, 1, 16, 128], P(None, 'prow', None, None, 'pcol'), may hold values from -0.125 to 0.125
- lower_two: float32 [3, 16, 128, 1, 16, 128], P(None, 'prow', None, None, 'pcol'), may hold values from -0.15625 to 0.15625
- dinv_one: float32 [1, 16, 128, 1, 16, 128], P(None, 'prow', None, None, 'pcol'), as said below
- dinv_two: float32 [1, 16, 128, 1, 16, 128], P(None, 'prow', None, None, 'pcol'), as said below
- seg_one: int32 [16], replicated, may hold values from 0 to 2, as said below
- seg_two: int32 [16], replicated, may hold values from 0 to 3, as said below
- parent_two: int32 [4], replicated, may hold values from 0 to 2
- pattern_one: int32 [3, 32], replicated, may hold values 0 or 1
- pattern_two: int32 [4, 48], replicated, may hold values 0 or 1
Outputs:
- inverse_one: float32 [1, 16, 128, 1, 16, 128], P(None, 'prow', None, None, 'pcol')
- inverse_two: float32 [1, 16, 128, 1, 16, 128], P(None, 'prow', None, None, 'pcol')
Inputs may be any that keep to these rules, and one draw needn't show every extreme that they name: `root_inverse`: Block-diagonal over supernodes is not implied; this is a symmetric matrix. `dinv_one`: Symmetric, and zero in every block whose row and column blocks belong to different supernodes of seg_one. `dinv_two`: Symmetric, and zero in every block whose row and column blocks belong to different supernodes of seg_two. `seg_one`: never falls; every supernode 0 to 2 has 1 to 8 consecutive blocks, one exactly 8. `seg_two`: never falls; every supernode 0 to 3 has 1 to 8 consecutive blocks, one exactly 8.
All inputs are finite; a program needn't handle non-finite values.
Results may differ from a plain program's by a relative error of at most 0.00005.
Values sent between devices are 32-bit elements; how exact they have to be, the bound alone decides.
A program may use at most 64 MiB of HBM per device.

v0:
```python
import jax
import jax.numpy as jnp
from jax import lax
from jax.sharding import PartitionSpec as P

highest = lax.Precision.HIGHEST


def contract(left_side, right_side):
    return lax.dot_general(
        left_side,
        right_side,
        (((0,), (0,)), ((), ())),
        precision=highest,
        preferred_element_type=jnp.float32,
    )


def flatten_local(blocks):
    squeezed = blocks[:, 0, :, :, 0, :]
    return squeezed.reshape(
        squeezed.shape[0] * squeezed.shape[1], squeezed.shape[2] * squeezed.shape[3]
    )


def to_blocks(matrix, block_width):
    return matrix.reshape(
        matrix.shape[0] // block_width,
        1,
        block_width,
        matrix.shape[1] // block_width,
        1,
        block_width,
    )


def apply_mask(matrix, block_mask, block_width):
    row_blocks = block_mask.shape[0]
    col_blocks = block_mask.shape[1]
    shaped = matrix.reshape(row_blocks, block_width, col_blocks, block_width)
    return (shaped * block_mask[:, None, :, None]).reshape(
        row_blocks * block_width, col_blocks * block_width
    )


def split_rows(matrix, pieces, block_width):
    return matrix.reshape(
        matrix.shape[0] // (pieces * block_width), pieces, block_width, matrix.shape[1]
    )


def merge_rows(blocks):
    return blocks.reshape(blocks.shape[0] * blocks.shape[1] * blocks.shape[2], blocks.shape[3])


def row_panel(gathered):
    picked = gathered[:, 0]
    return picked.reshape(
        picked.shape[0] * picked.shape[1], picked.shape[2] * picked.shape[3] * picked.shape[4]
    )


def same_mask(first_ids, second_ids):
    return (first_ids[:, None] == second_ids[None, :]).astype(jnp.float32)


def on_device(
    root_inverse,
    lower_one,
    lower_two,
    dinv_one,
    dinv_two,
    seg_one,
    seg_two,
    parent_two,
    pattern_one,
    pattern_two,
):
    block_width = root_inverse.shape[2]
    prow_total = lax.axis_size("prow")
    pcol_total = lax.axis_size("pcol")
    prow_place = lax.axis_index("prow")
    pcol_place = lax.axis_index("pcol")
    root_blocks = pattern_one.shape[1]
    first_nodes = pattern_one.shape[0]
    second_nodes = pattern_two.shape[0]

    def row_ids(amount):
        return jnp.arange(amount, dtype=jnp.int32) * prow_total + prow_place

    def col_ids(amount):
        return jnp.arange(amount, dtype=jnp.int32) * pcol_total + pcol_place

    root_rows = row_ids(root_inverse.shape[0])
    first_cols = col_ids(lower_one.shape[3])
    seg_cols = seg_one[first_cols]
    pick_first = same_mask(seg_cols, jnp.arange(first_nodes, dtype=jnp.int32))
    mask_one = jnp.dot(pick_first, pattern_one[:, root_rows].astype(jnp.float32)).T
    masked_one = apply_mask(flatten_local(lower_one), mask_one, block_width)
    second_rows = row_ids(lower_two.shape[0])
    second_cols = col_ids(lower_two.shape[3])
    seg_two_cols = seg_two[second_cols]
    parent_cols = parent_two[seg_two_cols]
    pick_second = same_mask(seg_two_cols, jnp.arange(second_nodes, dtype=jnp.int32))
    own_pattern = jnp.dot(pick_second, pattern_two[:, second_rows].astype(jnp.float32))
    pick_parent = same_mask(parent_cols, jnp.arange(first_nodes, dtype=jnp.int32))
    root_reach = jnp.dot(
        pick_parent, pattern_one[:, jnp.minimum(second_rows, root_blocks - 1)].astype(jnp.float32)
    )
    level_index = jnp.clip(second_rows - root_blocks, 0, seg_one.shape[0] - 1)
    level_reach = (seg_one[level_index][None, :] == parent_cols[:, None]).astype(jnp.float32)
    reachable = jnp.where((second_rows < root_blocks)[None, :], root_reach, level_reach)
    mask_two = (own_pattern * reachable).T
    masked_two = apply_mask(flatten_local(lower_two), mask_two, block_width)
    root_local = flatten_local(root_inverse)
    root_gathered, first_gathered, second_gathered = (
        lax.all_gather(root_inverse, "pcol", axis=4, tiled=True),
        lax.all_gather(to_blocks(masked_one, block_width), "pcol", axis=4, tiled=True),
        lax.all_gather(to_blocks(masked_two, block_width), "pcol", axis=4, tiled=True),
    )
    root_full = row_panel(root_gathered)
    first_full = row_panel(first_gathered)
    second_full = row_panel(second_gathered)
    turned_part = split_rows(contract(first_full, root_local), prow_total, block_width)
    solved_part = split_rows(contract(root_full, masked_one), prow_total, block_width)
    solved_blocks, turned_blocks = (
        lax.psum_scatter(solved_part, "prow", scatter_dimension=1, tiled=True),
        lax.psum_scatter(turned_part, "prow", scatter_dimension=1, tiled=True),
    )
    solved_one = merge_rows(solved_blocks)
    turned_one = merge_rows(turned_blocks)
    diag_part = split_rows(contract(first_full, solved_one), prow_total, block_width)
    diag_one = merge_rows(lax.psum_scatter(diag_part, "prow", scatter_dimension=1, tiled=True))
    same_one = same_mask(seg_one[row_ids(dinv_one.shape[0])], seg_one[col_ids(dinv_one.shape[3])])
    inverse_one = apply_mask(flatten_local(dinv_one) + diag_one, same_one, block_width)
    region = jnp.concatenate(
        [
            jnp.concatenate([root_local, -solved_one], axis=1),
            jnp.concatenate([-turned_one, inverse_one], axis=1),
        ],
        axis=0,
    )
    region_gathered = lax.all_gather(to_blocks(region, block_width), "pcol", axis=4, tiled=True)
    product_part = split_rows(
        contract(row_panel(region_gathered), masked_two), prow_total, block_width
    )
    solved_two = merge_rows(lax.psum_scatter(product_part, "prow", scatter_dimension=1, tiled=True))
    diag_two_part = split_rows(contract(second_full, solved_two), prow_total, block_width)
    diag_two = merge_rows(lax.psum_scatter(diag_two_part, "prow", scatter_dimension=1, tiled=True))
    same_two = same_mask(seg_two[row_ids(dinv_two.shape[0])], seg_two[col_ids(dinv_two.shape[3])])
    inverse_two = apply_mask(flatten_local(dinv_two) + diag_two, same_two, block_width)
    return (to_blocks(inverse_one, block_width), to_blocks(inverse_two, block_width))


def solution(mesh):
    return jax.shard_map(
        on_device,
        mesh=mesh,
        in_specs=(
            P(None, "prow", None, None, "pcol", None),
            P(None, "prow", None, None, "pcol", None),
            P(None, "prow", None, None, "pcol", None),
            P(None, "prow", None, None, "pcol", None),
            P(None, "prow", None, None, "pcol", None),
            P(),
            P(),
            P(),
            P(),
            P(),
        ),
        out_specs=(
            P(None, "prow", None, None, "pcol", None),
            P(None, "prow", None, None, "pcol", None),
        ),
        check_vma=False,
    )
```

profile of v0, /device:TPU:2, one launch (start us, length us, event | category | flops | bytes accessed | tf_op | source)
XLA Modules:
  0.0 629.4 jit_solution(16628335298792741638)
XLA Ops:
  7.2 1.7 copy.53
  10.3 1.4 fusion.23
  12.4 1.6 broadcast_multiply_fusion.1
  14.1 55.8 %all-gather.7.cloned.1.call-done = f32[2,1,128,2,16,128]{5,2,3,1,0,4:T(8,128)} async-done(((f32[2,1,128,2,1,128]{5,2,3,1,0,4:T(8,128)}), f32[2,1,128,2,16,128]{5,2,3,1,0,4:T(8,128)}) %all-gather.7.cloned.1.call-update) | async-done | bytes 4194320 | tf_op jit(solution)/shard_map/all_gather | solution.py:117
  70.0 6.6 %copy.54 = f32[2,1,128,2,16,128]{5,4,3,2,0,1:T(8,128)} copy(f32[2,1,128,2,16,128]{5,2,3,1,0,4:T(8,128)} %all-gather.7.cloned.1.call-done) | data formatting | bytes 8388608 | tf_op jit(solution)/shard_map/all_gather | solution.py:117
  76.6 5.0 reshape_squeeze.20
  81.6 4.5 convolution_bitcast_fusion.1
  86.5 1.9 copy.55
  88.7 33.1 %all-gather.5.cloned.1.call-done = f32[2,1,128,1,16,128]{5,2,3,1,0,4:T(8,128)} async-done(((f32[2,1,128,1,1,128]{5,2,3,1,0,4:T(8,128)}), f32[2,1,128,1,16,128]{5,2,3,1,0,4:T(8,128)}) %all-gather.5.cloned.1.call-update) | async-done | bytes 2097168 | tf_op jit(solution)/shard_map/all_gather | solution.py:118
  121.8 2.8 copy.51
  124.6 2.2 copy.79
  126.8 1.9 copy.52
  128.7 3.1 convolution_bitcast_fusion
  132.1 51.4 %reduce-scatter.8.cloned.1.call-done = f32[2,1,128,128]{3,2,0,1:T(8,128)} async-done(((f32[2,16,128,128]{3,2,0,1:T(8,128)}), f32[2,1,128,128]{3,2,0,1:T(8,128)}) %reduce-scatter.8.cloned.1.call-update) | async-done | bytes 131088 | tf_op jit(solution)/shard_map/reduce_scatter | solution.py:127
  183.4 3.8 convolution_bitcast_fusion.2
  188.6 54.9 %reduce-scatter.12.cloned.1.call-done = f32[1,1,128,256]{3,2,1,0:T(8,128)} async-done(((f32[1,16,128,256]{3,2,1,0:T(8,128)}), f32[1,1,128,256]{3,2,1,0:T(8,128)}) %reduce-scatter.12.cloned.1.call-update) | async-done | bytes 131088 | tf_op jit(solution)/shard_map/reduce_scatter | solution.py:128
  243.5 0.9 negate_bitcast_fusion
  244.4 57.2 %reduce-scatter.10.cloned.1.call-done = f32[1,1,128,128]{3,2,1,0:T(8,128)} async-done(((f32[1,16,128,128]{3,2,1,0:T(8,128)}), f32[1,1,128,128]{3,2,1,0:T(8,128)}) %reduce-scatter.10.cloned.1.call-update) | async-done | bytes 65552 | tf_op jit(solution)/shard_map/reduce_scatter | solution.py:133
  310.3 72.9 %all-gather.11.cloned.1.call-done = f32[3,1,128,3,16,128]{5,2,3,1,0,4:T(8,128)} async-done(((f32[3,1,128,3,1,128]{5,2,3,1,0,4:T(8,128)}), f32[3,1,128,3,16,128]{5,2,3,1,0,4:T(8,128)}) %all-gather.11.cloned.1.call-update) | async-done | bytes 9437200 | tf_op jit(solution)/shard_map/all_gather | solution.py:143
  383.2 12.8 %copy.63 = f32[3,1,128,3,16,128]{5,4,3,2,0,1:T(8,128)} copy(f32[3,1,128,3,16,128]{5,2,3,1,0,4:T(8,128)} %all-gather.11.cloned.1.call-done) | data formatting | bytes 18874368 | tf_op jit(solution)/shard_map/all_gather | solution.py:143
  395.9 10.0 %reshape_squeeze.24 = f32[384,6144]{1,0:T(8,128)} reshape(f32[3,1,128,3,16,128]{5,4,3,2,0,1:T(8,128)} %copy.63) | data formatting | bytes 18874368 | tf_op jit(solution)/shard_map/reshape;squeeze | solution.py:58
  406.0 9.6 %copy.64 = f32[6144,384]{1,0:T(8,128)} copy(f32[6144,384]{0,1:T(8,128)} %bitcast.148) | data formatting | bytes 18874368 | tf_op jit(solution)/shard_map/dot_general | solution.py:10
  415.6 11.0 %fusion.25 = f32[3,16,128,128]{3,2,1,0:T(8,128)} fusion(f32[3,16,128,384]{3,2,1,0:T(8,128)} %bitcast.149, f32[384,128,1,1]{1,0,3,2:T(8,128)S(1)} %bitcast.160), kind=kOutput, calls=%fused_computation.60 | convolution fusion | flops 3623878656 | bytes 12779520 | tf_op jit(solution)/shard_map/dot_general | solution.py:10
  427.9 10.0 %all-gather.9.cloned.1.call-done = f32[3,1,128,1,16,128]{5,2,3,1,0,4:T(8,128)} async-done(((f32[3,1,128,1,1,128]{5,2,3,1,0,4:T(8,128)}), f32[3,1,128,1,16,128]{5,2,3,1,0,4:T(8,128)}) %all-gather.9.cloned.1.call-update) | async-done | bytes 3145744 | tf_op jit(solution)/shard_map/all_gather | solution.py:119
  437.9 3.7 copy.60
  441.6 3.1 copy.78
  444.7 2.4 copy.61
  447.1 111.4 %all-reduce.3.cloned.1.call-done = f32[3,16,128,128]{3,2,1,0:T(8,128)} async-done(((f32[3,16,128,128]{3,2,1,0:T(8,128)}), f32[3,16,128,128]{3,2,1,0:T(8,128)}) %all-reduce.3.cloned.1.call-update) | async-done | bytes 3145744
  558.5 1.6 constant_dynamic-slice_fusion
  560.1 3.7 convolution_bitcast_fusion.3
  565.6 55.8 %reduce-scatter.14.cloned.1.call-done = f32[1,1,128,128]{3,2,1,0:T(8,128)} async-done(((f32[1,16,128,128]{3,2,1,0:T(8,128)}), f32[1,1,128,128]{3,2,1,0:T(8,128)}) %reduce-scatter.14.cloned.1.call-update) | async-done | bytes 65552 | tf_op jit(solution)/shard_map/reduce_scatter | solution.py:149
  621.4 1.5 fusion.2
  (70 shorter events, 12.0 us)
Async XLA Ops:
  7.2 62.8 %all-gather.7.cloned.1.call-start = ((), (), s32[]{:S(2)}) async-start(), calls=%async_computation.5 | async-start | bytes 4456448 | tf_op jit(solution)/shard_map/all_gather | solution.py:117
  8.9 112.9 %all-gather.5.cloned.1.call-start = ((), (), s32[]{:S(2)}) async-start(), calls=%async_computation.4 | async-start | bytes 2228224 | tf_op jit(solution)/shard_map/all_gather | solution.py:118
  14.1 169.4 %reduce-scatter.8.cloned.1.call-start = ((), (), s32[]{:S(2)}) async-start(), calls=%async_computation.6 | async-start | bytes 2228224 | tf_op jit(solution)/shard_map/reduce_scatter | solution.py:127
  76.6 5.0 copy-start.3
  86.5 2.0 copy-start.1
  88.4 155.1 %reduce-scatter.12.cloned.1.call-start = ((), (), s32[]{:S(2)}) async-start(), calls=%async_computation.9 | async-start | bytes 2228224 | tf_op jit(solution)/shard_map/reduce_scatter | solution.py:128
  131.8 169.7 %copy-start.5 = (f32[1,1,128,1,1,128]{5,4,3,2,1,0:T(1,128)S(1)}, f32[1,1,128,1,1,128]{5,4,3,2,1,0:T(1,128)}, u32[]{:S(2)}) copy-start(f32[1,1,128,1,1,128]{5,4,3,2,1,0:T(1,128)} %param.13) | copy-start | bytes 196612
  131.8 169.7 %reduce-scatter.10.cloned.1.call-start = ((), (), s32[]{:S(2)}) async-start(), calls=%async_computation.7 | async-start | bytes 1114112 | tf_op jit(solution)/shard_map/reduce_scatter | solution.py:133
  183.4 61.0 %copy-start.4 = (f32[2,1,128,128]{3,2,0,1:T(8,128)S(1)}, f32[2,1,128,128]{3,2,0,1:T(8,128)}, u32[]{:S(2)}) copy-start(f32[2,1,128,128]{3,2,0,1:T(8,128)} %reduce-scatter.8.cloned.1.call-done) | copy-start | bytes 393220
  187.2 118.2 %copy-start = (s32[16]{0:T(128)S(1)}, s32[16]{0:T(128)}, u32[]{:S(2)}) copy-start(s32[16]{0:T(128)} %param.15) | copy-start | bytes 196
  187.3 195.9 %all-gather.11.cloned.1.call-start = ((), (), s32[]{:S(2)}) async-start(), calls=%async_computation.10 | async-start | bytes 10027008 | tf_op jit(solution)/shard_map/all_gather | solution.py:143
  188.5 117.5 %copy-start.9 = (s32[4,48]{1,0:T(4,128)S(1)}, s32[4,48]{1,0:T(4,128)}, u32[]{:S(2)}) copy-start(s32[4,48]{1,0:T(4,128)} %param.19) | copy-start | bytes 2308
  188.5 118.2 %copy-start.10 = (s32[4]{0:T(128)S(1)}, s32[4]{0:T(128)}, u32[]{:S(2)}) copy-start(s32[4]{0:T(128)} %param.17) | copy-start | bytes 52
  188.6 120.9 %copy-start.7 = (f32[3,1,128,1,1,128]{5,4,3,2,1,0:T(1,128)S(1)}, f32[3,1,128,1,1,128]{5,4,3,2,1,0:T(1,128)}, u32[]{:S(2)}) copy-start(f32[3,1,128,1,1,128]{5,4,3,2,1,0:T(1,128)} %param.12) | copy-start | bytes 589828
  303.6 134.3 %all-gather.9.cloned.1.call-start = ((), (), s32[]{:S(2)}) async-start(), calls=%async_computation.8 | async-start | bytes 3342336 | tf_op jit(solution)/shard_map/all_gather | solution.py:119
  310.2 248.3 %all-reduce.3.cloned.1.call-start = ((), (), s32[]{:S(2)}) async-start(), calls=%async_computation.12 | async-start | bytes 6291456
  406.0 9.6 %copy-start.2 = (f32[3,1,128,1,1,128]{5,2,3,1,0,4:T(8,128)S(1)}, f32[3,1,128,1,1,128]{5,2,3,1,0,4:T(8,128)}, u32[]{:S(2)}) copy-start(f32[3,1,128,1,1,128]{5,2,3,1,0,4:T(8,128)} %broadcast_multiply_fusion) | copy-start | bytes 589828
  426.6 0.7 copy-start.11
  426.6 194.8 %reduce-scatter.14.cloned.1.call-start = ((), (), s32[]{:S(2)}) async-start(), calls=%async_computation.11 | async-start | bytes 1114112 | tf_op jit(solution)/shard_map/reduce_scatter | solution.py:149
  447.1 117.9 %copy-start.6 = (f32[1,1,128,128]{3,2,1,0:T(8,128)S(1)}, f32[1,1,128,128]{3,2,1,0:T(8,128)}, u32[]{:S(2)}) copy-start(f32[1,1,128,128]{3,2,1,0:T(8,128)} %reduce-scatter.10.cloned.1.call-done) | copy-start | bytes 196612
  447.1 174.3 %copy-start.8 = (f32[1,1,128,1,1,128]{5,4,3,2,1,0:T(1,128)S(1)}, f32[1,1,128,1,1,128]{5,4,3,2,1,0:T(1,128)}, u32[]{:S(2)}) copy-start(f32[1,1,128,1,1,128]{5,4,3,2,1,0:T(1,128)} %param.14) | copy-start | bytes 196612
Sparse Core Ops, SparseCore 0:
  10.4 59.4 all-gather.6
  72.4 49.3 all-gather.4
  124.3 59.0 reduce-scatter.7
  185.8 57.5 reduce-scatter.11
  245.8 55.7 reduce-scatter.9
  304.1 78.9 all-gather.10
  385.9 51.9 all-gather.8
  440.4 118.0 all-reduce.2
  564.0 57.4 reduce-scatter.13
where the time goes:
time: 630 us; the launch traced here: 629 us
  waiting for transfers between devices  503 us (80%)
  local copies, waits for them, and re-layouts  73.2 us (12%)
  matrix products  28.3 us (4%)
  between operations  18.2 us (3%)
  other arithmetic  6.39 us (1%)
    unnamed x10, waiting for transfers between devices  112 us
    all_gather x1, waiting for transfers between devices, on_device(): lax.all_gather(to_blocks(region, block_width), 'pcol', axis=4, tiled=True)  72.9 us
    reduce_scatter x1, waiting for transfers between devices, on_device(): lax.psum_scatter(diag_part, 'prow', scatter_dimension=1, tiled=True)  57.2 us
    all_gather x1, waiting for transfers between devices, on_device(): lax.all_gather(root_inverse, 'pcol', axis=4, tiled=True)  55.8 us
    reduce_scatter x1, waiting for transfers between devices, on_device(): lax.psum_scatter(diag_two_part, 'prow', scatter_dimension=1, tiled=True)  55.8 us
    reduce_scatter x1, waiting for transfers between devices, on_device(): lax.psum_scatter(turned_part, 'prow', scatter_dimension=1, tiled=True)  54.9 us
    reduce_scatter x1, waiting for transfers between devices, on_device(): lax.psum_scatter(solved_part, 'prow', scatter_dimension=1, tiled=True)  51.4 us
    all_gather x1, waiting for transfers between devices, on_device(): lax.all_gather(to_blocks(masked_one, block_width), 'pcol', axis=4, tiled=...  33.1 us
  transfers between devices with their start and end apart: 9, of which 9 were waited for; matrix products, arithmetic and copies ran while one was open for 15% of the time, Pallas kernels for 0%

commit v1 on v0

--- a/solution.py
+++ b/solution.py
@@ -140,7 +140,11 @@
         ],
         axis=0,
     )
-    region_gathered = lax.all_gather(to_blocks(region, block_width), "pcol", axis=4, tiled=True)
+    own = to_blocks(region, block_width)
+    size = lax.axis_size("pcol")
+    shards = jnp.stack([own for _ in range(size)])
+    shards = lax.all_to_all(shards, "pcol", split_axis=0, concat_axis=0)
+    region_gathered = jnp.concatenate(shards, axis=4)
     product_part = split_rows(
         contract(row_panel(region_gathered), masked_two), prow_total, block_width
     )

time: 630 us -> 700 us (1.11)
  waiting for transfers between devices: 503 us -> 560 us
  starting transfers between devices: 0.77 us -> 8.13 us
    all_to_all x0 -> x1, waiting for transfers between devices: none -> 138 us  [on_device(): shards = lax.all_to_all(shards, 'pcol', split_axis=0, concat_axis=0)]
    all_gather x1 -> x0, waiting for transfers between devices: 72.9 us -> none  [on_device(): lax.all_gather(to_blocks(region, block_width), 'pcol', axis=4, tiled=True)]
    all_gather x1 -> x0, local copies, waits for them, and re-layouts: 12.8 us -> none  [on_device(): lax.all_gather(to_blocks(region, block_width), 'pcol', axis=4, tiled=True)]
    reshape x2 -> x1, local copies, waits for them, and re-layouts: 1.1 us -> 12.8 us  [on_device(): region_gathered = jnp.concatenate(shards, axis=4)]
    all_gather x1, waiting for transfers between devices: 10 us -> 0.01 us  [on_device(): lax.all_gather(to_blocks(masked_two, block_width), 'pcol', axis=4, tiled=...]
    all_to_all x0 -> x1, starting transfers between devices: none -> 7.4 us  [on_device(): shards = lax.all_to_all(shards, 'pcol', split_axis=0, concat_axis=0)]
    unnamed x10 -> x9, waiting for transfers between devices: 112 us -> 114 us
  transfers between devices with their start and end apart: 9 -> 9, of which waited for: 9 -> 8; matrix products, arithmetic and copies ran while one was open for 15% -> 14% of each run, Pallas kernels for 0% -> 0%
where the time goes in v1:
time: 700 us; the launch traced here: 699 us
  waiting for transfers between devices  560 us (80%)
  local copies, waits for them, and re-layouts  77.1 us (11%)
  matrix products  28.4 us (4%)
  between operations  18.6 us (3%)
  starting transfers between devices  8.13 us (1%)
    all_to_all x1, waiting for transfers between devices, on_device(): shards = lax.all_to_all(shards, 'pcol', split_axis=0, concat_axis=0)  138 us
    unnamed x9, waiting for transfers between devices  114 us
    reduce_scatter x1, waiting for transfers between devices, on_device(): lax.psum_scatter(diag_part, 'prow', scatter_dimension=1, tiled=True)  57.2 us
    reduce_scatter x1, waiting for transfers between devices, on_device(): lax.psum_scatter(diag_two_part, 'prow', scatter_dimension=1, tiled=True)  55.7 us
    all_gather x1, waiting for transfers between devices, on_device(): lax.all_gather(root_inverse, 'pcol', axis=4, tiled=True)  55.7 us
    reduce_scatter x1, waiting for transfers between devices, on_device(): lax.psum_scatter(turned_part, 'prow', scatter_dimension=1, tiled=True)  54.9 us
    reduce_scatter x1, waiting for transfers between devices, on_device(): lax.psum_scatter(solved_part, 'prow', scatter_dimension=1, tiled=True)  51.3 us
    all_gather x1, waiting for transfers between devices, on_device(): lax.all_gather(to_blocks(masked_one, block_width), 'pcol', axis=4, tiled=...  33.1 us
  transfers between devices with their start and end apart: 9, of which 8 were waited for; matrix products, arithmetic and copies ran while one was open for 14% of the time, Pallas kernels for 0%

profile of v1, /device:TPU:2, one launch (start us, length us, event | category | flops | bytes accessed | tf_op | source)
XLA Modules:
  0.0 698.9 jit_solution(5657802204680895293)
XLA Ops:
  7.2 1.7 copy.69
  10.3 1.4 fusion.23
  12.5 1.6 broadcast_multiply_fusion.1
  14.2 55.7 %all-gather.6.cloned.1.call-done = f32[2,1,128,2,16,128]{5,2,3,1,0,4:T(8,128)} async-done(((f32[2,1,128,2,1,128]{5,2,3,1,0,4:T(8,128)}), f32[2,1,128,2,16,128]{5,2,3,1,0,4:T(8,128)}) %all-gather.6.cloned.1.call-update) | async-done | bytes 4194320 | tf_op jit(solution)/shard_map/all_gather | solution.py:117
  70.0 6.6 copy.70
  76.6 5.0 reshape_squeeze.17
  81.6 4.5 convolution_bitcast_fusion.1
  86.5 1.9 copy.71
  88.7 33.1 %all-gather.4.cloned.1.call-done = f32[2,1,128,1,16,128]{5,2,3,1,0,4:T(8,128)} async-done(((f32[2,1,128,1,1,128]{5,2,3,1,0,4:T(8,128)}), f32[2,1,128,1,16,128]{5,2,3,1,0,4:T(8,128)}) %all-gather.4.cloned.1.call-update) | async-done | bytes 2097168 | tf_op jit(solution)/shard_map/all_gather | solution.py:118
  121.8 2.8 copy.67
  124.6 2.2 copy.95
  126.8 1.9 copy.68
  128.7 3.1 convolution_bitcast_fusion
  132.1 51.3 %reduce-scatter.8.cloned.1.call-done = f32[2,1,128,128]{3,2,0,1:T(8,128)} async-done(((f32[2,16,128,128]{3,2,0,1:T(8,128)}), f32[2,1,128,128]{3,2,0,1:T(8,128)}) %reduce-scatter.8.cloned.1.call-update) | async-done | bytes 131088 | tf_op jit(solution)/shard_map/reduce_scatter | solution.py:127
  183.4 3.8 convolution_bitcast_fusion.2
  188.5 54.9 %reduce-scatter.12.cloned.1.call-done = f32[1,1,128,256]{3,2,1,0:T(8,128)} async-done(((f32[1,16,128,256]{3,2,1,0:T(8,128)}), f32[1,1,128,256]{3,2,1,0:T(8,128)}) %reduce-scatter.12.cloned.1.call-update) | async-done | bytes 131088 | tf_op jit(solution)/shard_map/reduce_scatter | solution.py:128
  244.4 57.2 %reduce-scatter.10.cloned.1.call-done = f32[1,1,128,128]{3,2,1,0:T(8,128)} async-done(((f32[1,16,128,128]{3,2,1,0:T(8,128)}), f32[1,1,128,128]{3,2,1,0:T(8,128)}) %reduce-scatter.10.cloned.1.call-update) | async-done | bytes 65552 | tf_op jit(solution)/shard_map/reduce_scatter | solution.py:133
  302.8 4.8 stack.3
  307.6 7.4 %all-to-all-start = ((f32[16,3,1,128,3,1,128]{6,3,5,4,2,1,0:T(8,128)}), f32[16,3,1,128,3,1,128]{6,3,5,4,2,1,0:T(8,128)}, u32[]{:S(2)}, u32[]{:S(2)}) async-start(f32[16,3,1,128,3,1,128]{6,3,5,4,2,1,0:T(8,128)} %stack.3), calls=%async_computation.3 | async-start | bytes 18874368 | tf_op jit(solution)/shard_map/all_to_all | solution.py:146
  321.6 138.2 %all-to-all-done = f32[16,3,1,128,3,1,128]{6,3,5,4,2,1,0:T(8,128)} async-done(((f32[16,3,1,128,3,1,128]{6,3,5,4,2,1,0:T(8,128)}), f32[16,3,1,128,3,1,128]{6,3,5,4,2,1,0:T(8,128)}, u32[]{:S(2)}, u32[]{:S(2)}) %all-to-all-start) | async-done | bytes 9437216 | tf_op jit(solution)/shard_map/all_to_all | solution.py:146
  459.8 12.8 %copy.79 = f32[3,1,128,3,16,1,128]{6,4,3,2,0,5,1:T(8,128)} copy(f32[3,1,128,3,16,1,128]{6,2,5,3,1,0,4:T(8,128)} %bitcast.41) | data formatting | bytes 18874368 | tf_op jit(solution)/shard_map/reshape | solution.py:147
  472.5 10.0 %reshape_squeeze_reshape.3 = f32[384,6144]{1,0:T(8,128)} reshape(f32[3,1,128,3,16,1,128]{6,4,3,2,0,5,1:T(8,128)} %copy.79) | data formatting | bytes 18874368 | tf_op jit(solution)/shard_map/reshape;squeeze;reshape | solution.py:58
  482.5 9.6 %copy.80 = f32[6144,384]{1,0:T(8,128)} copy(f32[6144,384]{0,1:T(8,128)} %bitcast.149) | data formatting | bytes 18874368 | tf_op jit(solution)/shard_map/dot_general | solution.py:10
  492.1 11.0 %fusion.25 = f32[3,16,128,128]{3,2,1,0:T(8,128)} fusion(f32[3,16,128,384]{3,2,1,0:T(8,128)} %bitcast.150, f32[384,128,1,1]{1,0,3,2:T(8,128)S(1)} %bitcast.161), kind=kOutput, calls=%fused_computation.60 | convolution fusion | flops 3623878656 | bytes 12779520 | tf_op jit(solution)/shard_map/dot_general | solution.py:10
  504.4 3.7 copy.76
  508.1 3.2 copy.94
  511.3 2.4 copy.77
  513.7 114.0 %all-reduce.3.cloned.1.call-done = f32[3,16,128,128]{3,2,1,0:T(8,128)} async-done(((f32[3,16,128,128]{3,2,1,0:T(8,128)}), f32[3,16,128,128]{3,2,1,0:T(8,128)}) %all-reduce.3.cloned.1.call-update) | async-done | bytes 3145744
  627.7 1.6 constant_dynamic-slice_fusion
  629.3 3.7 convolution_bitcast_fusion.3
  634.9 55.7 %reduce-scatter.14.cloned.1.call-done = f32[1,1,128,128]{3,2,1,0:T(8,128)} async-done(((f32[1,16,128,128]{3,2,1,0:T(8,128)}), f32[1,1,128,128]{3,2,1,0:T(8,128)}) %reduce-scatter.14.cloned.1.call-update) | async-done | bytes 65552 | tf_op jit(solution)/shard_map/reduce_scatter | solution.py:153
  690.6 1.5 fusion.2
  (70 shorter events, 12.0 us)
Async XLA Ops:
  7.2 62.8 %all-gather.6.cloned.1.call-start = ((), (), s32[]{:S(2)}) async-start(), calls=%async_computation.6 | async-start | bytes 4456448 | tf_op jit(solution)/shard_map/all_gather | solution.py:117
  8.9 112.9 %all-gather.4.cloned.1.call-start = ((), (), s32[]{:S(2)}) async-start(), calls=%async_computation.5 | async-start | bytes 2228224 | tf_op jit(solution)/shard_map/all_gather | solution.py:118
  14.2 169.3 %reduce-scatter.8.cloned.1.call-start = ((), (), s32[]{:S(2)}) async-start(), calls=%async_computation.7 | async-start | bytes 2228224 | tf_op jit(solution)/shard_map/reduce_scatter | solution.py:127
  76.6 5.0 copy-start.3
  86.5 2.0 copy-start.1
  88.4 155.1 %reduce-scatter.12.cloned.1.call-start = ((), (), s32[]{:S(2)}) async-start(), calls=%async_computation.10 | async-start | bytes 2228224 | tf_op jit(solution)/shard_map/reduce_scatter | solution.py:128
  131.8 169.7 %copy-start.5 = (f32[1,1,128,1,1,128]{5,4,3,2,1,0:T(1,128)S(1)}, f32[1,1,128,1,1,128]{5,4,3,2,1,0:T(1,128)}, u32[]{:S(2)}) copy-start(f32[1,1,128,1,1,128]{5,4,3,2,1,0:T(1,128)} %param.13) | copy-start | bytes 196612
  131.8 169.7 %reduce-scatter.10.cloned.1.call-start = ((), (), s32[]{:S(2)}) async-start(), calls=%async_computation.8 | async-start | bytes 1114112 | tf_op jit(solution)/shard_map/reduce_scatter | solution.py:133
  183.4 61.0 %copy-start.4 = (f32[2,1,128,128]{3,2,0,1:T(8,128)S(1)}, f32[2,1,128,128]{3,2,0,1:T(8,128)}, u32[]{:S(2)}) copy-start(f32[2,1,128,128]{3,2,0,1:T(8,128)} %reduce-scatter.8.cloned.1.call-done) | copy-start | bytes 393220
  307.6 9.2 %copy-start = (s32[16]{0:T(128)S(1)}, s32[16]{0:T(128)}, u32[]{:S(2)}) copy-start(s32[16]{0:T(128)} %param.15) | copy-start | bytes 196
  307.6 9.9 %copy-start.9 = (s32[4,48]{1,0:T(4,128)S(1)}, s32[4,48]{1,0:T(4,128)}, u32[]{:S(2)}) copy-start(s32[4,48]{1,0:T(4,128)} %param.19) | copy-start | bytes 2308
  307.6 10.5 %copy-start.10 = (s32[4]{0:T(128)S(1)}, s32[4]{0:T(128)}, u32[]{:S(2)}) copy-start(s32[4]{0:T(128)} %param.17) | copy-start | bytes 52
  307.6 13.1 %copy-start.7 = (f32[3,1,128,1,1,128]{5,4,3,2,1,0:T(1,128)S(1)}, f32[3,1,128,1,1,128]{5,4,3,2,1,0:T(1,128)}, u32[]{:S(2)}) copy-start(f32[3,1,128,1,1,128]{5,4,3,2,1,0:T(1,128)} %param.12) | copy-start | bytes 589828
  307.6 152.2 %all-to-all-start = ((f32[16,3,1,128,3,1,128]{6,3,5,4,2,1,0:T(8,128)}), f32[16,3,1,128,3,1,128]{6,3,5,4,2,1,0:T(8,128)}, u32[]{:S(2)}, u32[]{:S(2)}) async-start(f32[16,3,1,128,3,1,128]{6,3,5,4,2,1,0:T(8,128)} %stack.3), calls=%async_computation.3 | async-start | bytes 18874368 | tf_op jit(solution)/shard_map/all_to_all | solution.py:146
  315.0 189.4 %all-gather.8.cloned.1.call-start = ((), (), s32[]{:S(2)}) async-start(), calls=%async_computation.9 | async-start | bytes 3342336 | tf_op jit(solution)/shard_map/all_gather | solution.py:119
  321.5 306.2 %all-reduce.3.cloned.1.call-start = ((), (), s32[]{:S(2)}) async-start(), calls=%async_computation.12 | async-start | bytes 6291456
  482.5 9.6 %copy-start.2 = (f32[3,1,128,1,1,128]{5,2,3,1,0,4:T(8,128)S(1)}, f32[3,1,128,1,1,128]{5,2,3,1,0,4:T(8,128)}, u32[]{:S(2)}) copy-start(f32[3,1,128,1,1,128]{5,2,3,1,0,4:T(8,128)} %broadcast_multiply_fusion) | copy-start | bytes 589828
  503.1 0.7 copy-start.11
  503.2 187.4 %reduce-scatter.14.cloned.1.call-start = ((), (), s32[]{:S(2)}) async-start(), calls=%async_computation.11 | async-start | bytes 1114112 | tf_op jit(solution)/shard_map/reduce_scatter | solution.py:153
  513.7 120.6 %copy-start.6 = (f32[1,1,128,128]{3,2,1,0:T(8,128)S(1)}, f32[1,1,128,128]{3,2,1,0:T(8,128)}, u32[]{:S(2)}) copy-start(f32[1,1,128,128]{3,2,1,0:T(8,128)} %reduce-scatter.10.cloned.1.call-done) | copy-start | bytes 196612
  513.7 176.9 %copy-start.8 = (f32[1,1,128,1,1,128]{5,4,3,2,1,0:T(1,128)S(1)}, f32[1,1,128,1,1,128]{5,4,3,2,1,0:T(1,128)}, u32[]{:S(2)}) copy-start(f32[1,1,128,1,1,128]{5,4,3,2,1,0:T(1,128)} %param.14) | copy-start | bytes 196612
Sparse Core Ops, SparseCore 0:
  10.4 59.4 all-gather.5
  72.4 49.3 all-gather.3
  124.3 59.0 reduce-scatter.7
  185.8 57.5 reduce-scatter.11
  245.8 55.7 reduce-scatter.9
  321.6 136.1 all-gather.7
  503.3 124.3 all-reduce.2
  633.1 57.4 reduce-scatter.13
